TPU v7x, 32 devices: a whole 2x2x4 slice. The times are simulated.
32 devices in a mesh: mpo: 4 (over x, core), bond: 8 (over z, y).
Axes of the slice: x: 2, y: 2, z: 4, core: 2. Of those that a mesh axis runs over, the one named last changes fastest.
Arguments:
- environment: bfloat16 [4096, 40, 4096], P(None, 'mpo', 'bond'), may hold values from -60 to 60
- site_tensor: bfloat16 [4096, 4, 4096], P('bond'), may hold values from -0.09375 to 0.09375
- mpo_tensor: bfloat16 [40, 40, 4, 4], replicated, may hold values from -0.5 to 0.5
- sketch_site: bfloat16 [4096, 128], replicated, may hold values from -6 to 6
- sketch_expand: bfloat16 [128, 40, 4096], P('mpo'), may hold values from -60 to 60
- row_sectors: int32 [2, 4096, 4], P(None, 'bond'), may hold values from 0 to 5, as said below
- column_sectors: int32 [2, 128], replicated, may hold values from 0 to 5, as said below
Outputs:
- basis: bfloat16 [4096, 4, 128], P('bond')
- extended: float32 [128, 40, 128], P('bond', 'mpo')
Inputs may be any that keep to these rules, and one draw needn't show every extreme that they name: `row_sectors`: every joined row's label pair is (4, 0) or (5, 1); the rows labelled (5, 1) are one run of 64 consecutive joined rows (a, s) in the order a then s. `column_sectors`: every column's label pair is (4, 0) or (5, 1); exactly 16 columns are labelled (5, 1).
All inputs are finite; a program needn't handle non-finite values.
Results may differ from a plain program's by a relative error of at most 0.0064.
Values may be sent and summed in bfloat16 or wider, within the bound.
A program may use at most 128 MiB of HBM per device.

v0:
```python
import jax
import jax.numpy as jnp
from jax import lax
from jax.sharding import PartitionSpec as P

mixing = 0.5
shift_tolerance = 1e-06


def sector_mask(row_labels, column_labels):
    match = (row_labels[0][:, :, None] == column_labels[0][None, None, :]) & (
        row_labels[1][:, :, None] == column_labels[1][None, None, :]
    )
    return match.astype(jnp.float32)


def gram_of(left, right):
    column_count = left.shape[-1]
    return jnp.dot(
        left.reshape(-1, column_count).T,
        right.reshape(-1, column_count),
        precision=lax.Precision.HIGHEST,
        preferred_element_type=jnp.float32,
    )


def orthonormal(factor, values):
    column_count = values.shape[-1]
    solved = jax.scipy.linalg.solve_triangular(
        factor, values.reshape(-1, column_count).T, lower=True
    )
    return solved.T.reshape(values.shape).astype(jnp.bfloat16)


def body(
    environment, site_tensor, mpo_tensor, sketch_site, sketch_expand, row_sectors, column_sectors
):
    mpo_index = lax.axis_index("mpo")
    mpo_count = lax.axis_size("mpo")
    physical_width = environment.shape[1]
    local_rows = site_tensor.shape[0]
    physical = site_tensor.shape[1]
    column_count = column_sectors.shape[1]
    operator_rows = lax.dynamic_slice_in_dim(
        mpo_tensor, mpo_index * physical_width, physical_width, 0
    )
    sketched = jnp.einsum(
        "asb,kwb->wska", site_tensor, sketch_expand, preferred_element_type=jnp.float32
    ).astype(jnp.bfloat16)
    applied = jnp.einsum(
        "vwst,wtka->vska", mpo_tensor, sketched, preferred_element_type=jnp.float32
    ).astype(jnp.bfloat16)
    contracted = lax.all_to_all(applied, "mpo", split_axis=0, concat_axis=2, tiled=True)
    env_rows = environment
    expand_part = lax.psum_scatter(
        jnp.einsum("awc,wskc->ask", env_rows, contracted, preferred_element_type=jnp.float32),
        "bond",
        scatter_dimension=0,
        tiled=True,
    )
    mask_rows = sector_mask(row_sectors, column_sectors)
    share = local_rows // mpo_count
    offset = mpo_index * share
    expand_whole = lax.psum(expand_part, "mpo") * mask_rows
    site_whole = (
        jnp.dot(
            site_tensor.reshape(local_rows * physical, -1),
            sketch_site,
            preferred_element_type=jnp.float32,
        ).reshape(local_rows, physical, column_count)
        * mask_rows
    )
    part_site = lax.dynamic_slice_in_dim(site_whole, offset, share, 0)
    expansion_piece = lax.dynamic_slice_in_dim(expand_whole, offset, share, 0)
    square_site, square_expand = lax.psum(
        (jnp.sum(part_site * part_site), jnp.sum(expansion_piece * expansion_piece)),
        ("mpo", "bond"),
    )
    mix = mixing * jnp.sqrt((square_site + shift_tolerance) / (square_expand + shift_tolerance))
    combo_part = part_site + mix * expansion_piece
    gram_total = lax.psum(gram_of(combo_part, combo_part), ("mpo", "bond"))
    factor = jnp.linalg.cholesky(gram_total)
    basis_local = orthonormal(factor, site_whole + mix * expand_whole)
    flat_basis = basis_local.reshape(local_rows, physical * column_count)
    piece = lax.all_gather(basis_local, "bond", axis=0, tiled=True)
    env_rows = environment
    projected = jnp.einsum(
        "ax,awc->wxc",
        piece.reshape(piece.shape[0], -1),
        env_rows,
        preferred_element_type=jnp.float32,
    ).astype(jnp.bfloat16)
    couple_merged = jnp.einsum(
        "wxc,cy->wxy", projected, flat_basis, preferred_element_type=jnp.float32
    ).reshape(physical_width, physical, column_count, physical, column_count)
    boundary_share = jnp.einsum(
        "wvst,wsktl->kvl",
        operator_rows.astype(jnp.float32),
        couple_merged,
        precision=lax.Precision.HIGHEST,
    )
    reduced = lax.psum_scatter(boundary_share, "bond", scatter_dimension=0, tiled=True)
    extended = lax.psum_scatter(reduced, "mpo", scatter_dimension=1, tiled=True)
    return (basis_local, extended)


def solution(mesh):
    placed = (
        P(None, "mpo", "bond"),
        P("bond", None, None),
        P(),
        P(),
        P("mpo", None, None),
        P(None, "bond", None),
        P(),
    )
    return jax.shard_map(
        body,
        mesh=mesh,
        in_specs=placed,
        out_specs=(P("bond", None, None), P("bond", "mpo", None)),
        check_vma=False,
    )
```

profile of v0, /device:TPU:0, one launch (start us, length us, event | category | flops | bytes accessed | tf_op | source)
XLA Modules:
  0.0 739.9 jit_solution(15109001147891510651)
XLA Ops:
  7.2 31.3 %fusion.4 = bf16[32,40,512,4]{2,1,3,0:T(8,128)(2,1)} fusion(bf16[512,4,4096]{2,1,0:T(4,128)(2,1)} %param.8, bf16[32,40,4096]{2,1,0:T(8,128)(2,1)} %param.11), kind=kOutput, calls=%fused_computation.4 | convolution fusion | flops 21474836480 | bytes 32505856 | tf_op jit(solution)/shard_map/asb,kwb->wska/dot_general | solution.py:47
  38.5 4.6 fusion.13
  43.1 2.7 copy.35
  45.8 63.4 %all_to_all.18 = bf16[40,4,32,512]{3,1,2,0:T(4,128)(2,1)S(1)} all-to-all(bf16[40,4,32,512]{3,1,2,0:T(4,128)(2,1)S(1)} %copy.35), channel_id=1, replica_groups=mesh['mpo'=4,'bond'=8] {'mpo'}, dimensions={0} | all-to-all | bytes 10485760 | tf_op jit(solution)/shard_map/all_to_all | solution.py:53
  109.2 1.7 copy.36
  111.6 27.7 %fusion.10 = f32[4096,4,128]{2,0,1:T(8,128)} fusion(bf16[10,4,128,512]{3,2,0,1:T(8,128)(2,1)S(1)} %bitcast.100, bf16[4096,10,512]{2,0,1:T(8,128)(2,1)} %param.7), kind=kOutput, calls=%fused_computation.11 | convolution fusion | flops 21474836480 | bytes 55574528 | tf_op jit(solution)/shard_map/awc,wskc->ask/dot_general | solution.py:56
  139.4 148.3 %reduce-scatter.4.cloned.1.call-done = f32[512,4,128]{2,0,1:T(8,128)} async-done(((f32[4096,4,128]{2,0,1:T(8,128)}), f32[512,4,128]{2,0,1:T(8,128)}) %reduce-scatter.4.cloned.1.call-update) | async-done | bytes 1048592 | tf_op jit(solution)/shard_map/reduce_scatter | solution.py:55
  287.8 30.4 %fusion.22 = f32[512,4,128]{2,0,1:T(8,128)S(1)} fusion(bf16[512,4,4096]{2,1,0:T(4,128)(2,1)} %param.8, bf16[4096,128]{1,0:T(8,128)(2,1)S(1)} %copy-done, s32[128]{0:T(128)S(1)} %get-tuple-element.13, s32[512,4]{0,1:T(4,128)S(1)} %get-tuple-element.11, s32[128]{0:T(128)S(1)} %get-tuple-element.12, s32[512,4]{0,1:T(4,128)S(1)} %get-tuple-element.10), kind=kOutput, calls=%fused_computation.18 | convolution fusion | flops 2148532224 | bytes 18891776 | tf_op jit(solution)/shard_map/dot_general | solution.py:66
  318.9 6.6 all-reduce.4.cloned.1.call-done
  325.5 1.8 fusion.28
  327.9 40.0 %all-reduce = (f32[]{:T(128)}, f32[]{:T(128)}) all-reduce(f32[]{:T(128)} %multiply_reduce_fusion.1, f32[]{:T(128)} %multiply_reduce_fusion), channel_id=1, replica_groups=mesh['mpo'=4,'bond'=8] {'mpo','bond'}, use_global_device_ids=true, to_apply=%region_1.0 | all-reduce | flops 2 | bytes 16 | tf_op jit(solution)/shard_map/psum | solution.py:75
  369.3 1.2 convolution_bitcast_fusion
  370.8 119.7 %all-reduce.6.cloned.1.call-done = f32[128,128]{0,1:T(8,128)} async-done(((f32[128,128]{0,1:T(8,128)}), f32[128,128]{0,1:T(8,128)}) %all-reduce.6.cloned.1.call-update) | async-done | bytes 65552 | tf_op jit(solution)/shard_map/psum | solution.py:81
  492.3 11.7 %cholesky.16 = f32[128,128]{1,0:T(8,128)S(1)} custom-call(f32[128,128]{1,0:T(8,128)S(1)} %fusion.41), custom_call_target="Cholesky" | custom-call | tf_op jit(solution)/shard_map/jit(cholesky)/cholesky | solution.py:82
  505.4 9.8 %custom-call.7 = f32[1,128,128]{1,2,0:T(8,128)S(1)} custom-call(f32[1,128,128]{2,1,0:T(8,128)S(1)} %fusion.38), custom_call_target="InvertDiagBlocksLowerTriangular" | custom-call | tf_op jit(solution)/shard_map/jit(_solve_triangular)/triangular_solve | solution.py:29
  515.2 2.0 convolution_convert_fusion.1
  517.3 75.9 %all-gather.2.cloned.1.call-done = bf16[4096,4,128]{0,2,1:T(8,128)(2,1)} async-done(((bf16[512,4,128]{0,2,1:T(8,128)(2,1)}), bf16[4096,4,128]{0,2,1:T(8,128)(2,1)}) %all-gather.2.cloned.1.call-update) | async-done | bytes 4194320 | tf_op jit(solution)/shard_map/all_gather | solution.py:85
  593.2 27.9 %convolution_convert_fusion = bf16[512,10,512]{2,0,1:T(8,128)(2,1)S(1)} fusion(bf16[4096,512,1]{0,1,2:T(8,128)(2,1)} %bitcast.101, bf16[4096,10,512]{2,0,1:T(8,128)(2,1)} %param.7), kind=kOutput, calls=%fused_computation.16 | convolution fusion | flops 21477457920 | bytes 51380224 | tf_op jit(solution)/shard_map/ax,awc->wxc/dot_general | solution.py:87
  621.1 2.9 fusion.29
  624.0 16.9 %fusion.19 = f32[128,40,128]{2,1,0:T(8,128)} fusion(f32[10,4,128,4,128]{4,2,3,1,0:T(8,128)S(1)} %fusion.29, bf16[40,40,4,4]{1,0,3,2:T(8,128)(2,1)S(1)} %copy.34, s32[]{:T(128)S(6)} %select_n.13), kind=kOutput, calls=%fused_computation.17 | convolution fusion | flops 1258291200 | bytes 13172740 | tf_op jit(solution)/shard_map/wvst,wsktl->kvl/dot_general | solution.py:96
  640.9 69.2 %reduce-scatter.6.cloned.1.call-done = f32[16,40,128]{2,1,0:T(8,128)} async-done(((f32[128,40,128]{2,1,0:T(8,128)}), f32[16,40,128]{2,1,0:T(8,128)}) %reduce-scatter.6.cloned.1.call-update) | async-done | bytes 327696 | tf_op jit(solution)/shard_map/reduce_scatter | solution.py:102
  710.2 1.7 copy.45
  711.9 1.1 copy.46
  713.0 19.7 %reduce-scatter.8.cloned.1.call-done = f32[16,10,128]{2,0,1:T(8,128)} async-done(((f32[16,40,128]{2,0,1:T(8,128)}), f32[16,10,128]{2,0,1:T(8,128)}) %reduce-scatter.8.cloned.1.call-update) | async-done | bytes 81936 | tf_op jit(solution)/shard_map/reduce_scatter | solution.py:103
  (33 shorter events, 5.7 us)
Async XLA Ops:
  7.2 280.6 %copy-start = (bf16[4096,128]{1,0:T(8,128)(2,1)S(1)}, bf16[4096,128]{1,0:T(8,128)(2,1)}, u32[]{:S(2)}) copy-start(bf16[4096,128]{1,0:T(8,128)(2,1)} %param.10) | copy-start | bytes 3145732
  7.2 31.4 %copy-start.2 = (bf16[40,40,4,4]{1,3,2,0:T(4,128)(2,1)S(1)}, bf16[40,40,4,4]{1,3,2,0:T(4,128)(2,1)}, u32[]{:S(2)}) copy-start(bf16[40,40,4,4]{1,3,2,0:T(4,128)(2,1)} %param.9) | copy-start | bytes 153604
  7.2 280.5 %reduce-scatter.4.cloned.1.call-start = ((), (), s32[]{:S(2)}) async-start(), calls=%async_computation.4 | async-start | bytes 9437184 | tf_op jit(solution)/shard_map/reduce_scatter | solution.py:55
  111.6 27.8 %copy-start.4 = (s32[2,128]{1,0:T(2,128)S(1)}, s32[2,128]{1,0:T(2,128)}, u32[]{:S(2)}) copy-start(s32[2,128]{1,0:T(2,128)} %param.13) | copy-start | bytes 3076
  111.6 27.8 %copy-start.3 = (s32[2,512,4]{1,2,0:T(4,128)S(1)}, s32[2,512,4]{1,2,0:T(4,128)}, u32[]{:S(2)}) copy-start(s32[2,512,4]{1,2,0:T(4,128)} %param.12) | copy-start | bytes 49156
  139.3 186.1 %all-reduce.4.cloned.1.call-start = ((), (), s32[]{:S(2)}) async-start(), calls=%async_computation.5 | async-start | bytes 2097152 | tf_op jit(solution)/shard_map/psum | solution.py:64
  287.7 202.8 %all-reduce.6.cloned.1.call-start = ((), (), s32[]{:S(2)}) async-start(), calls=%async_computation.6 | async-start | bytes 131072 | tf_op jit(solution)/shard_map/psum | solution.py:81
  370.6 222.6 %all-gather.2.cloned.1.call-start = ((), (), s32[]{:S(2)}) async-start(), calls=%async_computation.7 | async-start | bytes 4718592 | tf_op jit(solution)/shard_map/all_gather | solution.py:85
  517.2 193.0 %reduce-scatter.6.cloned.1.call-start = ((), (), s32[]{:S(2)}) async-start(), calls=%async_computation.8 | async-start | bytes 2949120 | tf_op jit(solution)/shard_map/reduce_scatter | solution.py:102
  593.2 27.9 %copy-start.1 = (bf16[512,4,128]{0,2,1:T(8,128)(2,1)S(1)}, bf16[512,4,128]{0,2,1:T(8,128)(2,1)}, u32[]{:S(2)}) copy-start(bf16[512,4,128]{0,2,1:T(8,128)(2,1)} %convolution_convert_fusion.1) | copy-start | bytes 1572868
  640.9 91.8 %reduce-scatter.8.cloned.1.call-start = ((), (), s32[]{:S(2)}) async-start(), calls=%async_computation.9 | async-start | bytes 409600 | tf_op jit(solution)/shard_map/reduce_scatter | solution.py:103
Sparse Core Ops, SparseCore 0:
  139.5 148.2 reduce-scatter.3
  290.1 35.3 all-reduce.3
  370.7 119.7 all-reduce.5
  517.3 75.8 all-gather.1
  641.0 69.0 reduce-scatter.5
  713.1 19.5 reduce-scatter.7
where the time goes:
time: 749 us; the launch traced here: 740 us
  waiting for transfers between devices  439 us (59%)
  matrix products  145 us (19%)
  blocking collectives  103 us (14%)
  other arithmetic  26.8 us (4%)
  between operations  16.1 us (2%)
  local copies, waits for them, and re-layouts  8.83 us (1%)
    reduce_scatter x1, waiting for transfers between devices, body(): lax.psum_scatter(jnp.einsum('awc,wskc->ask', env_rows, contracted, prefer...  148 us
    psum x1, waiting for transfers between devices, body(): gram_total = lax.psum(gram_of(combo_part, combo_part), ('mpo', 'bond'))  120 us
    all_gather x1, waiting for transfers between devices, body(): piece = lax.all_gather(basis_local, 'bond', axis=0, tiled=True)  75.9 us
    reduce_scatter x1, waiting for transfers between devices, body(): lax.psum_scatter(boundary_share, 'bond', scatter_dimension=0, tiled=True)  69.2 us
    all_to_all x1, blocking collectives, body(): lax.all_to_all(applied, 'mpo', split_axis=0, concat_axis=2, tiled=True)  63.4 us
    psum x1, blocking collectives, body(): lax.psum((jnp.sum(part_site * part_site), jnp.sum(expansion_piece * expan...  40 us
    dot_general x1, matrix products, body(): jnp.einsum('asb,kwb->wska', site_tensor, sketch_expand, preferred_element...  31.3 us
    dot_general x1, matrix products, body(): jnp.dot(site_tensor.reshape(local_rows * physical, -1), sketch_site, pref...  30.4 us
  transfers between devices with their start and end apart: 6, of which 6 were waited for; matrix products, arithmetic and copies ran while one was open for 4% of the time, Pallas kernels for 0%

commit v1 on v0

--- a/solution.py
+++ b/solution.py
@@ -5,6 +5,15 @@
 
 mixing = 0.5
 shift_tolerance = 1e-06
+lay_groups_over_axis = lambda local_values: jnp.concatenate(
+    lax.all_to_all(
+        jnp.stack(jnp.split(local_values, lax.axis_size("mpo"), axis=0), axis=0),
+        axis_name="mpo",
+        split_axis=0,
+        concat_axis=0,
+    ),
+    axis=2,
+)
 
 
 def sector_mask(row_labels, column_labels):
@@ -50,7 +59,7 @@
     applied = jnp.einsum(
         "vwst,wtka->vska", mpo_tensor, sketched, preferred_element_type=jnp.float32
     ).astype(jnp.bfloat16)
-    contracted = lax.all_to_all(applied, "mpo", split_axis=0, concat_axis=2, tiled=True)
+    contracted = lay_groups_over_axis(applied)
     env_rows = environment
     expand_part = lax.psum_scatter(
         jnp.einsum("awc,wskc->ask", env_rows, contracted, preferred_element_type=jnp.float32),

time: 749 us -> 753 us (level)
  no operation moved by 1% of the time
where the time goes in v1:
time: 753 us; the launch traced here: 744 us
  waiting for transfers between devices  439 us (58%)
  matrix products  145 us (19%)
  blocking collectives  103 us (14%)
  other arithmetic  28.4 us (4%)
  between operations  16.1 us (2%)
  local copies, waits for them, and re-layouts  11.5 us (2%)
    reduce_scatter x1, waiting for transfers between devices, body(): lax.psum_scatter(jnp.einsum('awc,wskc->ask', env_rows, contracted, prefer...  148 us
    psum x1, waiting for transfers between devices, body(): gram_total = lax.psum(gram_of(combo_part, combo_part), ('mpo', 'bond'))  120 us
    all_gather x1, waiting for transfers between devices, body(): piece = lax.all_gather(basis_local, 'bond', axis=0, tiled=True)  75.9 us
    reduce_scatter x1, waiting for transfers between devices, body(): lax.psum_scatter(boundary_share, 'bond', scatter_dimension=0, tiled=True)  69.4 us
    all_to_all x1, blocking collectives, lax.all_to_all(jnp.stack(jnp.split(local_values, lax.axis_size('mpo'), ax...  63.4 us
    psum x1, blocking collectives, body(): lax.psum((jnp.sum(part_site * part_site), jnp.sum(expansion_piece * expan...  40 us
    dot_general x1, matrix products, body(): jnp.einsum('asb,kwb->wska', site_tensor, sketch_expand, preferred_element...  31.3 us
    dot_general x1, matrix products, body(): jnp.dot(site_tensor.reshape(local_rows * physical, -1), sketch_site, pref...  30.4 us
  transfers between devices with their start and end apart: 6, of which 6 were waited for; matrix products, arithmetic and copies ran while one was open for 4% of the time, Pallas kernels for 0%

profile of v1, /device:TPU:0, one launch (start us, length us, event | category | flops | bytes accessed | tf_op | source)
XLA Modules:
  0.0 743.8 jit_solution(2658797177516635998)
XLA Ops:
  7.2 31.3 %fusion.4 = bf16[32,40,512,4]{2,1,3,0:T(8,128)(2,1)} fusion(bf16[512,4,4096,1]{2,1,0,3:T(4,128)(2,1)} %bitcast.105, bf16[32,40,4096]{2,1,0:T(8,128)(2,1)} %param.11), kind=kOutput, calls=%fused_computation.4 | convolution fusion | flops 21474836480 | bytes 32505856 | tf_op jit(solution)/shard_map/asb,kwb->wska/dot_general | solution.py:56
  38.6 4.6 fusion.12
  43.2 3.4 slice_bitcast_fusion.3
  46.6 1.6 pad_maximum_fusion
  48.2 3.0 copy.22
  51.2 63.4 %all_to_all.5 = bf16[4,10,4,32,512]{4,3,2,1,0:T(8,128)(2,1)S(1)} all-to-all(bf16[4,10,4,32,512]{4,3,2,1,0:T(8,128)(2,1)S(1)} %copy.22), channel_id=1, replica_groups=mesh['mpo'=4,'bond'=8] {'mpo'}, dimensions={0} | all-to-all | bytes 10485760 | tf_op jit(solution)/shard_map/all_to_all | solution.py:9
  115.2 27.7 %fusion.9 = f32[4096,4,128]{2,0,1:T(8,128)} fusion(bf16[10,4,128,512]{3,2,0,1:T(8,128)(2,1)S(1)} %bitcast.104, bf16[4096,10,512]{2,0,1:T(8,128)(2,1)} %param.7), kind=kOutput, calls=%fused_computation.11 | convolution fusion | flops 21474836480 | bytes 55574528 | tf_op jit(solution)/shard_map/awc,wskc->ask/dot_general | solution.py:65
  143.7 147.7 %reduce-scatter.4.cloned.1.call-done = f32[512,4,128]{2,0,1:T(8,128)} async-done(((f32[4096,4,128]{2,0,1:T(8,128)}), f32[512,4,128]{2,0,1:T(8,128)}) %reduce-scatter.4.cloned.1.call-update) | async-done | bytes 1048592 | tf_op jit(solution)/shard_map/reduce_scatter | solution.py:64
  291.4 30.4 %fusion.21 = f32[512,4,128]{2,0,1:T(8,128)S(1)} fusion(bf16[512,4,4096]{2,1,0:T(4,128)(2,1)} %param.8, bf16[4096,128]{1,0:T(8,128)(2,1)S(1)} %copy-done, s32[128]{0:T(128)S(1)} %get-tuple-element.15, s32[512,4]{0,1:T(4,128)S(1)} %get-tuple-element.13, s32[128]{0:T(128)S(1)} %get-tuple-element.14, s32[512,4]{0,1:T(4,128)S(1)} %get-tuple-element.12), kind=kOutput, calls=%fused_computation.22 | convolution fusion | flops 2148532224 | bytes 18891776 | tf_op jit(solution)/shard_map/dot_general | solution.py:75
  322.5 6.6 all-reduce.4.cloned.1.call-done
  329.1 1.8 fusion.27
  331.6 40.0 %all-reduce = (f32[]{:T(128)}, f32[]{:T(128)}) all-reduce(f32[]{:T(128)} %multiply_reduce_fusion.1, f32[]{:T(128)} %multiply_reduce_fusion), channel_id=1, replica_groups=mesh['mpo'=4,'bond'=8] {'mpo','bond'}, use_global_device_ids=true, to_apply=%region_1.0 | all-reduce | flops 2 | bytes 16 | tf_op jit(solution)/shard_map/psum | solution.py:84
  373.0 1.2 convolution_bitcast_fusion
  374.4 119.7 %all-reduce.6.cloned.1.call-done = f32[128,128]{0,1:T(8,128)} async-done(((f32[128,128]{0,1:T(8,128)}), f32[128,128]{0,1:T(8,128)}) %all-reduce.6.cloned.1.call-update) | async-done | bytes 65552 | tf_op jit(solution)/shard_map/psum | solution.py:90
  496.0 11.7 %cholesky.16 = f32[128,128]{1,0:T(8,128)S(1)} custom-call(f32[128,128]{1,0:T(8,128)S(1)} %fusion.40), custom_call_target="Cholesky" | custom-call | tf_op jit(solution)/shard_map/jit(cholesky)/cholesky | solution.py:91
  509.0 9.8 %custom-call.7 = f32[1,128,128]{1,2,0:T(8,128)S(1)} custom-call(f32[1,128,128]{2,1,0:T(8,128)S(1)} %fusion.37), custom_call_target="InvertDiagBlocksLowerTriangular" | custom-call | tf_op jit(solution)/shard_map/jit(_solve_triangular)/triangular_solve | solution.py:38
  518.8 2.0 convolution_convert_fusion.1
  520.9 75.9 %all-gather.2.cloned.1.call-done = bf16[4096,4,128]{0,2,1:T(8,128)(2,1)} async-done(((bf16[512,4,128]{0,2,1:T(8,128)(2,1)}), bf16[4096,4,128]{0,2,1:T(8,128)(2,1)}) %all-gather.2.cloned.1.call-update) | async-done | bytes 4194320 | tf_op jit(solution)/shard_map/all_gather | solution.py:94
  596.9 27.9 %convolution_convert_fusion = bf16[512,10,512]{2,0,1:T(8,128)(2,1)S(1)} fusion(bf16[4096,512,1]{0,1,2:T(8,128)(2,1)} %bitcast.106, bf16[4096,10,512]{2,0,1:T(8,128)(2,1)} %param.7), kind=kOutput, calls=%fused_computation.16 | convolution fusion | flops 21477457920 | bytes 51380224 | tf_op jit(solution)/shard_map/ax,awc->wxc/dot_general | solution.py:96
  624.8 2.9 fusion.28
  627.7 16.9 %fusion.18 = f32[128,40,128]{2,1,0:T(8,128)} fusion(f32[10,4,128,4,128]{4,2,3,1,0:T(8,128)S(1)} %fusion.28, bf16[40,40,4,4]{1,0,3,2:T(8,128)(2,1)S(1)} %copy.21, s32[]{:T(128)S(6)} %select_n.13), kind=kOutput, calls=%fused_computation.21 | convolution fusion | flops 1258291200 | bytes 13172740 | tf_op jit(solution)/shard_map/wvst,wsktl->kvl/dot_general | solution.py:105
  644.6 69.4 %reduce-scatter.6.cloned.1.call-done = f32[16,40,128]{2,1,0:T(8,128)} async-done(((f32[128,40,128]{2,1,0:T(8,128)}), f32[16,40,128]{2,1,0:T(8,128)}) %reduce-scatter.6.cloned.1.call-update) | async-done | bytes 327696 | tf_op jit(solution)/shard_map/reduce_scatter | solution.py:111
  714.0 1.7 copy.30
  716.8 19.7 %reduce-scatter.8.cloned.1.call-done = f32[16,10,128]{2,0,1:T(8,128)} async-done(((f32[16,40,128]{2,0,1:T(8,128)}), f32[16,10,128]{2,0,1:T(8,128)}) %reduce-scatter.8.cloned.1.call-update) | async-done | bytes 81936 | tf_op jit(solution)/shard_map/reduce_scatter | solution.py:112
  (34 shorter events, 7.4 us)
Async XLA Ops:
  7.2 284.3 %copy-start = (bf16[4096,128]{1,0:T(8,128)(2,1)S(1)}, bf16[4096,128]{1,0:T(8,128)(2,1)}, u32[]{:S(2)}) copy-start(bf16[4096,128]{1,0:T(8,128)(2,1)} %param.10) | copy-start | bytes 3145732
  7.2 284.2 %reduce-scatter.4.cloned.1.call-start = ((), (), s32[]{:S(2)}) async-start(), calls=%async_computation.4 | async-start | bytes 9437184 | tf_op jit(solution)/shard_map/reduce_scatter | solution.py:64
  7.2 31.4 %copy-start.2 = (bf16[40,40,4,4]{1,3,2,0:T(4,128)(2,1)S(1)}, bf16[40,40,4,4]{1,3,2,0:T(4,128)(2,1)}, u32[]{:S(2)}) copy-start(bf16[40,40,4,4]{1,3,2,0:T(4,128)(2,1)} %param.9) | copy-start | bytes 153604
  143.0 0.7 copy-start.4
  143.0 0.7 copy-start.3
  143.0 186.1 %all-reduce.4.cloned.1.call-start = ((), (), s32[]{:S(2)}) async-start(), calls=%async_computation.5 | async-start | bytes 2097152 | tf_op jit(solution)/shard_map/psum | solution.py:73
  291.4 202.8 %all-reduce.6.cloned.1.call-start = ((), (), s32[]{:S(2)}) async-start(), calls=%async_computation.6 | async-start | bytes 131072 | tf_op jit(solution)/shard_map/psum | solution.py:90
  374.2 222.6 %all-gather.2.cloned.1.call-start = ((), (), s32[]{:S(2)}) async-start(), calls=%async_computation.7 | async-start | bytes 4718592 | tf_op jit(solution)/shard_map/all_gather | solution.py:94
  520.8 193.2 %reduce-scatter.6.cloned.1.call-start = ((), (), s32[]{:S(2)}) async-start(), calls=%async_computation.8 | async-start | bytes 2949120 | tf_op jit(solution)/shard_map/reduce_scatter | solution.py:111
  596.9 27.9 %copy-start.1 = (bf16[512,4,128]{0,2,1:T(8,128)(2,1)S(1)}, bf16[512,4,128]{0,2,1:T(8,128)(2,1)}, u32[]{:S(2)}) copy-start(bf16[512,4,128]{0,2,1:T(8,128)(2,1)} %convolution_convert_fusion.1) | copy-start | bytes 1572868
  644.6 91.9 %reduce-scatter.8.cloned.1.call-start = ((), (), s32[]{:S(2)}) async-start(), calls=%async_computation.9 | async-start | bytes 409600 | tf_op jit(solution)/shard_map/reduce_scatter | solution.py:112
Sparse Core Ops, SparseCore 0:
  143.1 148.2 reduce-scatter.3
  293.7 35.3 all-reduce.3
  374.3 119.7 all-reduce.5
  521.0 75.8 all-gather.1
  644.7 69.2 reduce-scatter.5
  716.9 19.5 reduce-scatter.7
